TPU v7x, 32 devices: a whole 2x2x4 slice. The times are simulated.
32 devices in a mesh: refl: 4 (over y, x), grid: 8 (over z, core).
Axes of the slice: x: 2, y: 2, z: 4, core: 2. Of those that a mesh axis runs over, the one named last changes fastest.
Arguments:
- density: bfloat16 [2, 256, 256, 256], P(None, 'grid'), may hold values from -6 to 6
- displacement: bfloat16 [3, 256, 256, 256], P(None, 'grid'), may hold values from -0.8984375 to 0.8984375
- support: int32 [256, 256, 256], P('grid'), may hold values 0 or 1
- millers: int32 [4, 3], replicated, may hold values from -3 to 3
- amplitude: float32 [4, 256, 256, 256], P('refl', None, 'grid'), may hold values from 0.1 to 3
Outputs:
- grad_density: float32 [2, 256, 256, 256], P(None, 'grid', 'refl')
- grad_displacement: float32 [3, 256, 256, 256], P(None, 'grid', 'refl')
All inputs are finite; a program needn't handle non-finite values. No bound on the sum of `support` on one device may be relied on, other than what follows from the above.
Results may differ from a plain program's by a relative error of at most 0.00065.
Values sent between devices are 32-bit elements; how exact they have to be, the bound alone decides.
A program may use at most 192 MiB of HBM per device.

v0:
```python
import math
import jax
import jax.numpy as jnp
from jax import lax
from jax.sharding import PartitionSpec as P


def dft_tables(length):
    counter = jnp.arange(length, dtype=jnp.int32)
    product = counter[:, None] * counter[None, :] % length
    angles = product.astype(jnp.float32) * (2.0 * math.pi / length)
    factor = 1.0 / math.sqrt(length)
    return (jnp.cos(angles) * factor, jnp.sin(angles) * factor)


def transform_axis(real_part, imag_part, pattern, tables, inverse):
    cosine, sine = tables
    real_cos = jnp.einsum(pattern, real_part, cosine, precision=lax.Precision.HIGHEST)
    real_sin = jnp.einsum(pattern, real_part, sine, precision=lax.Precision.HIGHEST)
    imag_cos = jnp.einsum(pattern, imag_part, cosine, precision=lax.Precision.HIGHEST)
    imag_sin = jnp.einsum(pattern, imag_part, sine, precision=lax.Precision.HIGHEST)
    if inverse:
        return (real_cos - imag_sin, imag_cos + real_sin)
    return (real_cos + imag_sin, imag_cos - real_sin)


def phase_terms(hkl_rows, shift):
    angle = (
        2.0
        * math.pi
        * jnp.einsum("gc,cxyz->gxyz", hkl_rows, shift, precision=lax.Precision.HIGHEST)
    )
    return (jnp.cos(angle), jnp.sin(angle))


def gradient_terms(hkl_rows, mask, rho_real, rho_imag, cosine, sine, back_real, back_imag):
    obj_real = mask * (rho_real * cosine - rho_imag * sine)
    obj_imag = mask * (rho_real * sine + rho_imag * cosine)
    grad_real = jnp.sum(mask * (cosine * back_real + sine * back_imag), axis=0)
    grad_imag = jnp.sum(mask * (cosine * back_imag - sine * back_real), axis=0)
    twist = obj_real * back_imag - obj_imag * back_real
    grad_shift = jnp.einsum("gc,gxyz->cxyz", hkl_rows, twist, precision=lax.Precision.HIGHEST)
    return (jnp.stack([grad_real, grad_imag]), grad_shift)


def body(density, displacement, support, millers, amplitude):
    local_refl = amplitude.shape[0]
    total_refl = millers.shape[0]
    full_x = amplitude.shape[1]
    full_y = support.shape[1]
    full_z = support.shape[2]
    rho_real = density[0].astype(jnp.float32)
    rho_imag = density[1].astype(jnp.float32)
    shift = displacement.astype(jnp.float32)
    mask = support.astype(jnp.float32)
    indices = millers.astype(jnp.float32)
    table_x = dft_tables(full_x)
    table_y = dft_tables(full_y)
    table_z = dft_tables(full_z)
    first_refl = lax.axis_index("refl") * local_refl
    own_hkl = lax.dynamic_slice_in_dim(indices, first_refl, local_refl, 0)
    cosine, sine = phase_terms(own_hkl, shift)
    obj_real = mask * (rho_real * cosine - rho_imag * sine)
    obj_imag = mask * (rho_real * sine + rho_imag * cosine)
    real_part, imag_part = transform_axis(obj_real[0], obj_imag[0], "xyz,zk->xyk", table_z, False)
    real_part, imag_part = transform_axis(real_part, imag_part, "xyz,yk->xkz", table_y, False)
    columns = lax.all_to_all(
        jnp.stack([real_part, imag_part]), "grid", split_axis=2, concat_axis=1, tiled=True
    )
    spec_real, spec_imag = transform_axis(columns[0], columns[1], "xyz,xk->kyz", table_x, False)
    magnitude = jnp.sqrt(spec_real * spec_real + spec_imag * spec_imag)
    ratio = amplitude[0] / jnp.maximum(magnitude, 0.5)
    resid_real = spec_real - ratio * spec_real
    resid_imag = spec_imag - ratio * spec_imag
    real_part, imag_part = transform_axis(resid_real, resid_imag, "xyz,xk->kyz", table_x, True)
    slabs = lax.all_to_all(
        jnp.stack([real_part, imag_part]), "grid", split_axis=1, concat_axis=2, tiled=True
    )
    real_part, imag_part = transform_axis(slabs[0], slabs[1], "xyz,yk->xkz", table_y, True)
    real_part, imag_part = transform_axis(real_part, imag_part, "xyz,zk->xyk", table_z, True)
    back_reals = [real_part]
    back_imags = [imag_part]
    back_real = jnp.stack(back_reals)
    back_imag = jnp.stack(back_imags)
    scale = 1.0 / total_refl
    grad_rho, grad_shift = gradient_terms(
        own_hkl, mask, rho_real, rho_imag, cosine, sine, back_real, back_imag
    )
    grad_rho, grad_shift = (
        lax.psum_scatter(grad_rho, "refl", scatter_dimension=2, tiled=True),
        lax.psum_scatter(grad_shift, "refl", scatter_dimension=2, tiled=True),
    )
    return (grad_rho * scale, grad_shift * scale)


def solution(mesh):
    in_specs = (
        P(None, "grid", None, None),
        P(None, "grid", None, None),
        P("grid", None, None),
        P(),
        P("refl", None, "grid", None),
    )
    out_specs = (P(None, "grid", "refl", None), P(None, "grid", "refl", None))
    return jax.shard_map(body, mesh=mesh, in_specs=in_specs, out_specs=out_specs, check_vma=False)
```

profile of v0, /device:TPU:0, one launch (start us, length us, event | category | flops | bytes accessed | tf_op | source)
XLA Modules:
  0.0 1654.8 jit_solution(4140846365251873728)
XLA Ops:
  7.2 0.7 convert_element_type.71
  7.9 62.4 %fusion = f32[1,32,256,256]{3,0,2,1:T(1,128)} fusion(bf16[3,32,256,256]{3,2,1,0:T(8,128)(2,1)} %param.6, f32[4,3]{1,0:T(4,128)S(1)} %convert_element_type.71, s32[]{:T(128)S(6)} %select_n.60), kind=kOutput, calls=%fused_computation.5 | convolution fusion | flops 75497472 | bytes 20972036 | tf_op jit(solution)/shard_map/gc,cxyz->gxyz/dot_general | solution.py:31
  70.2 34.3 %fusion.3 = (f32[32,256,256]{2,1,0:T(8,128)S(1)}, f32[32,256,256]{2,1,0:T(8,128)S(1)}) fusion(s32[32,256,256]{2,1,0:T(8,128)S(1)} %copy-done.4, f32[1,32,256,256]{3,0,2,1:T(1,128)} %fusion, bf16[2,32,256,256]{3,2,1,0:T(8,128)(2,1)} %param.5), kind=kLoop, calls=%fused_computation.15 | loop fusion | flops 25165824 | bytes 41943040 | tf_op jit(solution)/shard_map/mul | solution.py:63
  104.6 7.9 fusion.68
  112.5 8.6 fusion.57
  121.0 8.3 fusion.55
  129.3 10.8 fusion.70
  140.2 11.6 fusion.22
  151.7 11.7 fusion.20
  163.5 17.8 %add_bitcast_fusion.1 = f32[1,32,256,256]{3,2,1,0:T(8,128)} fusion(f32[256,32,256]{2,0,1:T(8,128)} %fusion.22, f32[32,256,256]{2,1,0:T(8,128)} %fusion.70, f32[32,256,256]{2,1,0:T(8,128)S(1)} %fusion.57), kind=kOutput, calls=%fused_computation.34 | convolution fusion | flops 6447628288 | bytes 33554432 | tf_op jit(solution)/shard_map/xyz,yk->xkz/dot_general | solution.py:18
  181.3 18.4 %subtract_bitcast_fusion.1 = f32[1,32,256,256]{3,2,1,0:T(8,128)} fusion(f32[256,32,256]{2,0,1:T(8,128)} %fusion.20, f32[32,256,256]{2,1,0:T(8,128)} %fusion.70, f32[32,256,256]{2,1,0:T(8,128)S(1)} %fusion.57), kind=kOutput, calls=%fused_computation.33 | convolution fusion | flops 6447628288 | bytes 33554432 | tf_op jit(solution)/shard_map/xyz,yk->xkz/dot_general | solution.py:19
  199.7 6.9 pad_maximum_fusion
  206.6 17.6 %copy.32 = f32[2,32,256,256]{3,1,0,2:T(8,128)S(1)} copy(f32[2,32,256,256]{3,2,1,0:T(8,128)S(1)} %pad_maximum_fusion) | data formatting | bytes 33554432 | tf_op jit(solution)/shard_map/stack | solution.py:68
  224.2 370.7 %all_to_all.30 = f32[2,32,256,256]{3,1,0,2:T(8,128)S(1)} all-to-all(f32[2,32,256,256]{3,1,0,2:T(8,128)S(1)} %copy.32), channel_id=1, replica_groups=mesh['refl'=4,'grid'=8] {'grid'}, dimensions={2} | all-to-all | bytes 33554432 | tf_op jit(solution)/shard_map/all_to_all | solution.py:67
  594.9 6.0 copy.117
  601.0 6.8 fusion.205
  607.7 11.7 fusion.47
  619.4 11.6 fusion.73
  631.0 11.9 fusion.49
  642.9 23.2 %multiply_subtract_fusion.1 = (f32[256,32,256]{2,0,1:T(8,128)S(1)}, f32[256,32,256]{2,0,1:T(8,128)S(1)}) fusion(f32[1,256,32,256]{3,2,1,0:T(8,128)} %param.9, f32[256,32,256]{2,0,1:T(8,128)} %fusion.47, f32[256,32,256]{2,0,1:T(8,128)} %fusion.73, f32[256,32,256]{2,0,1:T(8,128)} %fusion.49, f32[256,32,256]{2,0,1:T(8,128)} %bitcast.191), kind=kOutput, calls=%fused_computation.9 | convolution fusion | flops 6466502656 | bytes 58720256 | tf_op jit(solution)/shard_map/xyz,xk->kyz/dot_general | solution.py:20
  666.1 12.1 fusion.75
  678.2 11.7 fusion.61
  689.9 14.1 subtract_bitcast_fusion
  703.9 14.1 add_bitcast_fusion
  718.0 4.9 pad_maximum_fusion.1
  722.9 20.2 %copy.43 = f32[2,256,32,256]{3,2,0,1:T(8,128)} copy(f32[2,256,32,256]{3,1,2,0:T(8,128)S(1)} %pad_maximum_fusion.1) | data formatting | bytes 33554432 | tf_op jit(solution)/shard_map/stack | solution.py:77
  743.2 5.7 all-to-all-start.1
  748.9 0.0 reduce-scatter.3.cloned.1.call-start
  749.0 1.0 fusion.232
  749.9 362.6 %all-to-all-done.1 = f32[2,256,32,256]{3,2,0,1:T(8,128)} async-done(((f32[2,256,32,256]{3,2,0,1:T(8,128)}), f32[2,256,32,256]{3,2,0,1:T(8,128)}, u32[]{:S(2)}, u32[]{:S(2)}) %all-to-all-start.1) | async-done | bytes 16777248 | tf_op jit(solution)/shard_map/all_to_all | solution.py:76
  1112.5 11.9 copy.116
  1124.4 7.9 fusion.204
  1132.4 8.6 fusion.41
  1141.0 8.8 fusion.59
  1149.9 10.8 fusion.6
  1160.7 11.0 fusion.8
  1171.8 11.7 fusion.43
  1183.4 14.2 fusion.77
  1197.6 15.6 fusion.32
  1213.3 43.5 %multiply_bitcast_fusion.1 = (f32[1,32,256,256]{3,2,1,0:T(8,128)S(1)}, f32[1,32,256,256]{3,2,1,0:T(8,128)S(1)}, f32[32,256,256]{2,1,0:T(8,128)}) fusion(f32[32,256,256]{2,1,0:T(8,128)} %fusion.32, s32[32,256,256]{2,1,0:T(8,128)} %param.7, f32[1,32,256,256]{3,0,2,1:T(1,128)} %fusion, f32[32,256,256]{2,1,0:T(8,128)S(1)} %bitcast.189, ...), kind=kOutput, calls=%fused_computation.30 | convolution fusion | flops 6473908224 | bytes 92536832 | tf_op jit(solution)/shard_map/xyz,zk->xyk/dot_general | solution.py:19
  1256.7 6.4 pad_maximum_fusion.2
  1263.1 0.0 reduce-scatter.5.cloned.1.call-start
  1263.2 0.7 fusion.107
  1263.9 12.6 broadcast_multiply_fusion
  1276.5 139.5 %reduce-scatter.3.cloned.1.call-done = f32[2,32,64,256]{3,2,1,0:T(8,128)} async-done(((f32[2,32,256,256]{3,2,1,0:T(8,128)}), f32[2,32,64,256]{3,2,1,0:T(8,128)}) %reduce-scatter.3.cloned.1.call-update) | async-done | bytes 4194320 | tf_op jit(solution)/shard_map/reduce_scatter | solution.py:90
  1416.0 4.8 broadcast_multiply_fusion.2
  1420.8 220.1 %reduce-scatter.5.cloned.1.call-done = f32[3,32,64,256]{3,2,1,0:T(8,128)} async-done(((f32[3,32,256,256]{3,2,1,0:T(8,128)}), f32[3,32,64,256]{3,2,1,0:T(8,128)}) %reduce-scatter.5.cloned.1.call-update) | async-done | bytes 6291472 | tf_op jit(solution)/shard_map/reduce_scatter | solution.py:91
  1640.8 6.6 broadcast_multiply_fusion.1
  (26 shorter events, 0.1 us)
Async XLA Ops:
  7.9 62.4 %copy-start.6 = (f32[4,3]{1,0:T(4,128)}, f32[4,3]{1,0:T(4,128)S(1)}, u32[]{:S(2)}) copy-start(f32[4,3]{1,0:T(4,128)S(1)} %convert_element_type.71) | copy-start | bytes 148
  7.9 62.4 %copy-start.4 = (s32[32,256,256]{2,1,0:T(8,128)S(1)}, s32[32,256,256]{2,1,0:T(8,128)}, u32[]{:S(2)}) copy-start(s32[32,256,256]{2,1,0:T(8,128)} %param.7) | copy-start | bytes 25165828
  104.5 7.9 copy-start.1
  104.5 24.8 %copy-start = (f32[32,256,256]{2,1,0:T(8,128)}, f32[32,256,256]{2,1,0:T(8,128)S(1)}, u32[]{:S(2)}) copy-start(f32[32,256,256]{2,1,0:T(8,128)S(1)} %get-tuple-element.6) | copy-start | bytes 25165828
  607.7 23.3 %copy-start.2 = (f32[1,8,32,32,256]{4,2,1,3,0:T(8,128)}, f32[1,8,32,32,256]{4,2,1,3,0:T(8,128)S(1)}, u32[]{:S(2)}) copy-start(f32[1,8,32,32,256]{4,2,1,3,0:T(8,128)S(1)} %get-tuple-element.12) | copy-start | bytes 25165828
  703.9 14.1 copy-start.5
  743.2 369.4 %all-to-all-start.1 = ((f32[2,256,32,256]{3,2,0,1:T(8,128)}), f32[2,256,32,256]{3,2,0,1:T(8,128)}, u32[]{:S(2)}, u32[]{:S(2)}) async-start(f32[2,256,32,256]{3,2,0,1:T(8,128)} %copy.43), calls=%async_computation.1 | async-start | bytes 33554432 | tf_op jit(solution)/shard_map/all_to_all | solution.py:76
  748.9 667.0 %reduce-scatter.3.cloned.1.call-start = ((), (), s32[]{:S(2)}) async-start(), calls=%async_computation.4 | async-start | bytes 20971520 | tf_op jit(solution)/shard_map/reduce_scatter | solution.py:90
  1132.4 8.7 copy-start.3
  1183.4 29.8 %slice-start = ((s8[8388608]{0:T(1024)(128)(4,1)}), s8[4194304]{0:T(1024)(128)(4,1)S(1)}, s32[]{:S(2)}) async-start(s8[8388608]{0:T(1024)(128)(4,1)} %bitcast.186), calls=%async_computation.6 | async-start | bytes 8388608
  1183.4 29.8 %slice-start.2 = ((s8[8388608]{0:T(1024)(128)(4,1)}), s8[4194304]{0:T(1024)(128)(4,1)S(1)}, s32[]{:S(2)}) async-start(s8[8388608]{0:T(1024)(128)(4,1)} %bitcast.188), calls=%async_computation.8 | async-start | bytes 8388608
  1197.6 15.6 slice-start.1
  1197.6 15.6 slice-start.3
  1263.1 377.7 %reduce-scatter.5.cloned.1.call-start = ((), (), s32[]{:S(2)}) async-start(), calls=%async_computation.5 | async-start | bytes 31457280 | tf_op jit(solution)/shard_map/reduce_scatter | solution.py:91
Sparse Core Ops, SparseCore 0:
  1263.3 152.6 reduce-scatter.2
  1419.1 221.7 reduce-scatter.4
where the time goes:
time: 1660 us; the launch traced here: 1650 us
  waiting for transfers between devices  722 us (43%)
  matrix products  392 us (24%)
  blocking collectives  371 us (22%)
  other arithmetic  78.1 us (5%)
  local copies, waits for them, and re-layouts  71.2 us (4%)
    all_to_all x1, blocking collectives, body(): lax.all_to_all(jnp.stack([real_part, imag_part]), 'grid', split_axis=2, c...  371 us
    all_to_all x1, waiting for transfers between devices, body(): lax.all_to_all(jnp.stack([real_part, imag_part]), 'grid', split_axis=1, c...  363 us
    reduce_scatter x1, waiting for transfers between devices, body(): lax.psum_scatter(grad_shift, 'refl', scatter_dimension=2, tiled=True)  220 us
    reduce_scatter x1, waiting for transfers between devices, body(): lax.psum_scatter(grad_rho, 'refl', scatter_dimension=2, tiled=True)  139 us
    dot_general x6, matrix products, transform_axis(): jnp.einsum(pattern, real_part, sine, precision=lax.Precision.HIGHEST)  105 us
    dot_general x6, matrix products, transform_axis(): jnp.einsum(pattern, real_part, cosine, precision=lax.Precision.HIGHEST)  82.2 us
    dot_general x6, matrix products, transform_axis(): jnp.einsum(pattern, imag_part, cosine, precision=lax.Precision.HIGHEST)  74.2 us
    dot_general x6, matrix products, transform_axis(): jnp.einsum(pattern, imag_part, sine, precision=lax.Precision.HIGHEST)  68.7 us
  transfers between devices with their start and end apart: 3, of which 3 were waited for; matrix products, arithmetic and copies ran while one was open for 1% of the time, Pallas kernels for 0%

commit v1 on v0

--- a/solution.py
+++ b/solution.py
@@ -73,8 +73,14 @@
     resid_real = spec_real - ratio * spec_real
     resid_imag = spec_imag - ratio * spec_imag
     real_part, imag_part = transform_axis(resid_real, resid_imag, "xyz,xk->kyz", table_x, True)
-    slabs = lax.all_to_all(
-        jnp.stack([real_part, imag_part]), "grid", split_axis=1, concat_axis=2, tiled=True
+    slabs = jnp.concatenate(
+        lax.all_to_all(
+            jnp.stack(jnp.split(jnp.stack([real_part, imag_part]), lax.axis_size("grid"), axis=1)),
+            "grid",
+            0,
+            0,
+        ),
+        axis=2,
     )
     real_part, imag_part = transform_axis(slabs[0], slabs[1], "xyz,yk->xkz", table_y, True)
     real_part, imag_part = transform_axis(real_part, imag_part, "xyz,zk->xyk", table_z, True)

time: 1660 us -> 1620 us (0.976)
  local copies, waits for them, and re-layouts: 71.2 us -> 38.9 us
    dot_general x1, matrix products: 62.4 us -> 37 us  [phase_terms(): jnp.einsum('gc,cxyz->gxyz', hkl_rows, shift, precision=lax.Precision.HIGH...]
    another operation x2 -> x1, local copies, waits for them, and re-layouts: 37.9 us -> 17.6 us  [body(): jnp.stack([real_part, imag_part])]
where the time goes in v1:
time: 1620 us; the launch traced here: 1610 us
  waiting for transfers between devices  722 us (45%)
  matrix products  376 us (23%)
  blocking collectives  371 us (23%)
  other arithmetic  84.6 us (5%)
  local copies, waits for them, and re-layouts  38.9 us (2%)
    all_to_all x1, blocking collectives, body(): lax.all_to_all(jnp.stack([real_part, imag_part]), 'grid', split_axis=2, c...  371 us
    all_to_all x1, waiting for transfers between devices, body(): lax.all_to_all(jnp.stack(jnp.split(jnp.stack([real_part, imag_part]), lax...  363 us
    reduce_scatter x1, waiting for transfers between devices, body(): lax.psum_scatter(grad_shift, 'refl', scatter_dimension=2, tiled=True)  220 us
    reduce_scatter x1, waiting for transfers between devices, body(): lax.psum_scatter(grad_rho, 'refl', scatter_dimension=2, tiled=True)  139 us
    dot_general x6, matrix products, transform_axis(): jnp.einsum(pattern, real_part, sine, precision=lax.Precision.HIGHEST)  107 us
    dot_general x6, matrix products, transform_axis(): jnp.einsum(pattern, real_part, cosine, precision=lax.Precision.HIGHEST)  82.5 us
    dot_general x6, matrix products, transform_axis(): jnp.einsum(pattern, imag_part, cosine, precision=lax.Precision.HIGHEST)  78.4 us
    dot_general x6, matrix products, transform_axis(): jnp.einsum(pattern, imag_part, sine, precision=lax.Precision.HIGHEST)  71 us
  transfers between devices with their start and end apart: 3, of which 3 were waited for; matrix products, arithmetic and copies ran while one was open for 1% of the time, Pallas kernels for 0%

profile of v1, /device:TPU:0, one launch (start us, length us, event | category | flops | bytes accessed | tf_op | source)
XLA Modules:
  0.0 1613.6 jit_solution(15317771073000106770)
XLA Ops:
  7.9 37.0 %fusion = f32[1,32,256,256]{3,0,2,1:T(1,128)S(1)} fusion(bf16[3,32,256,256]{3,2,1,0:T(8,128)(2,1)} %param.6, f32[4,3]{1,0:T(4,128)S(1)} %convert_element_type.71, s32[]{:T(128)S(6)} %select_n.60), kind=kOutput, calls=%fused_computation.17 | convolution fusion | flops 75497472 | bytes 20972036 | tf_op jit(solution)/shard_map/gc,cxyz->gxyz/dot_general | solution.py:31
  44.9 34.0 %fusion.3 = (f32[32,256,256]{2,1,0:T(8,128)S(1)}, f32[32,256,256]{2,1,0:T(8,128)S(1)}) fusion(s32[32,256,256]{2,1,0:T(8,128)S(1)} %copy-done.7, f32[1,32,256,256]{3,0,2,1:T(1,128)S(1)} %fusion, bf16[2,32,256,256]{3,2,1,0:T(8,128)(2,1)} %param.5), kind=kLoop, calls=%fused_computation.27 | loop fusion | flops 25165824 | bytes 41943040 | tf_op jit(solution)/shard_map/mul | solution.py:63
  79.0 7.9 fusion.96
  86.9 8.3 fusion.86
  95.2 8.5 fusion.84
  103.8 10.8 fusion.98
  114.6 11.6 fusion.30
  126.2 11.7 fusion.28
  137.9 17.8 %add_bitcast_fusion.1 = f32[1,32,256,256]{3,2,1,0:T(8,128)} fusion(f32[256,32,256]{2,0,1:T(8,128)} %fusion.30, f32[32,256,256]{2,1,0:T(8,128)} %fusion.98, f32[32,256,256]{2,1,0:T(8,128)S(1)} %fusion.86), kind=kOutput, calls=%fused_computation.46 | convolution fusion | flops 6447628288 | bytes 33554432 | tf_op jit(solution)/shard_map/xyz,yk->xkz/dot_general | solution.py:18
  155.6 18.1 %subtract_bitcast_fusion.1 = f32[1,32,256,256]{3,2,1,0:T(8,128)} fusion(f32[256,32,256]{2,0,1:T(8,128)} %fusion.28, f32[32,256,256]{2,1,0:T(8,128)} %fusion.98, f32[32,256,256]{2,1,0:T(8,128)S(1)} %fusion.86), kind=kOutput, calls=%fused_computation.45 | convolution fusion | flops 6447628288 | bytes 33554432 | tf_op jit(solution)/shard_map/xyz,yk->xkz/dot_general | solution.py:19
  173.8 6.9 pad_maximum_fusion
  180.6 17.6 %copy.34 = f32[2,32,256,256]{3,1,0,2:T(8,128)S(1)} copy(f32[2,32,256,256]{3,2,1,0:T(8,128)S(1)} %pad_maximum_fusion) | data formatting | bytes 33554432 | tf_op jit(solution)/shard_map/stack | solution.py:68
  198.3 371.0 %all_to_all.20 = f32[2,32,256,256]{3,1,0,2:T(8,128)S(1)} all-to-all(f32[2,32,256,256]{3,1,0,2:T(8,128)S(1)} %copy.34), channel_id=1, replica_groups=mesh['refl'=4,'grid'=8] {'grid'}, dimensions={2} | all-to-all | bytes 33554432 | tf_op jit(solution)/shard_map/all_to_all | solution.py:67
  569.3 6.1 copy.127
  575.3 6.8 fusion.232
  582.1 11.7 fusion.101
  593.8 11.6 fusion.76
  605.5 11.9 fusion.78
  617.4 23.2 %multiply_subtract_fusion = (f32[256,32,256]{2,0,1:T(8,128)S(1)}, f32[256,32,256]{2,0,1:T(8,128)S(1)}) fusion(f32[1,256,32,256]{3,2,1,0:T(8,128)} %param.9, f32[256,32,256]{2,0,1:T(8,128)} %fusion.76, f32[256,32,256]{2,0,1:T(8,128)} %fusion.101, f32[256,32,256]{2,0,1:T(8,128)} %fusion.78, f32[256,32,256]{2,0,1:T(8,128)} %bitcast.216), kind=kOutput, calls=%fused_computation.20 | convolution fusion | flops 6466502656 | bytes 58720256 | tf_op jit(solution)/shard_map/xyz,xk->kyz/dot_general | solution.py:20
  640.5 12.0 fusion.89
  652.5 11.8 fusion.103
  664.2 12.8 add_bitcast_fusion
  677.1 13.7 subtract_bitcast_fusion
  690.8 1.5 fusion.51
  692.3 1.5 fusion.54
  693.8 1.4 fusion.57
  695.2 1.5 fusion.60
  696.7 1.4 fusion.63
  698.1 1.5 fusion.66
  699.6 1.4 fusion.48
  701.0 1.5 fusion.68
  702.5 5.8 all-to-all-start.1
  709.4 362.6 %all-to-all-done.1 = f32[8,2,32,32,256]{4,2,3,1,0:T(8,128)} async-done(((f32[8,2,32,32,256]{4,2,3,1,0:T(8,128)}), f32[8,2,32,32,256]{4,2,3,1,0:T(8,128)}, u32[]{:S(2)}, u32[]{:S(2)}) %all-to-all-start.1) | async-done | bytes 16777248 | tf_op jit(solution)/shard_map/all_to_all | solution.py:77
  1072.0 7.7 fusion.231
  1079.7 12.9 fusion.14
  1092.6 12.8 fusion.18
  1105.4 10.8 fusion.6
  1116.2 10.8 fusion.8
  1127.1 14.7 fusion.16
  1141.8 14.8 fusion.20
  1156.6 15.6 fusion.40
  1172.3 43.4 %multiply_bitcast_fusion.1 = (f32[1,32,256,256]{3,2,1,0:T(8,128)S(1)}, f32[1,32,256,256]{3,2,1,0:T(8,128)S(1)}, f32[32,256,256]{2,1,0:T(8,128)}) fusion(f32[32,256,256]{2,1,0:T(8,128)} %fusion.40, s32[32,256,256]{2,1,0:T(8,128)} %param.7, f32[1,32,256,256]{3,0,2,1:T(1,128)} %copy-done.8, f32[32,256,256]{2,1,0:T(8,128)S(1)} %bitcast.214, ...), kind=kOutput, calls=%fused_computation.42 | convolution fusion | flops 6473908224 | bytes 92536832 | tf_op jit(solution)/shard_map/xyz,zk->xyk/dot_general | solution.py:19
  1215.7 6.4 pad_maximum_fusion.1
  1222.8 12.6 broadcast_multiply_fusion
  1235.4 139.5 %reduce-scatter.3.cloned.1.call-done = f32[2,32,64,256]{3,2,1,0:T(8,128)} async-done(((f32[2,32,256,256]{3,2,1,0:T(8,128)}), f32[2,32,64,256]{3,2,1,0:T(8,128)}) %reduce-scatter.3.cloned.1.call-update) | async-done | bytes 4194320 | tf_op jit(solution)/shard_map/reduce_scatter | solution.py:96
  1374.9 4.8 broadcast_multiply_fusion.2
  1379.7 220.1 %reduce-scatter.5.cloned.1.call-done = f32[3,32,64,256]{3,2,1,0:T(8,128)} async-done(((f32[3,32,256,256]{3,2,1,0:T(8,128)}), f32[3,32,64,256]{3,2,1,0:T(8,128)}) %reduce-scatter.5.cloned.1.call-update) | async-done | bytes 6291472 | tf_op jit(solution)/shard_map/reduce_scatter | solution.py:97
  1599.7 6.6 broadcast_multiply_fusion.1
  (42 shorter events, 2.5 us)
Async XLA Ops:
  7.9 37.0 %copy-start.9 = (f32[4,3]{1,0:T(4,128)}, f32[4,3]{1,0:T(4,128)S(1)}, u32[]{:S(2)}) copy-start(f32[4,3]{1,0:T(4,128)S(1)} %convert_element_type.71) | copy-start | bytes 148
  7.9 37.0 %copy-start.7 = (s32[32,256,256]{2,1,0:T(8,128)S(1)}, s32[32,256,256]{2,1,0:T(8,128)}, u32[]{:S(2)}) copy-start(s32[32,256,256]{2,1,0:T(8,128)} %param.7) | copy-start | bytes 25165828
  44.9 34.0 %copy-start.8 = (f32[1,32,256,256]{3,0,2,1:T(1,128)}, f32[1,32,256,256]{3,0,2,1:T(1,128)S(1)}, u32[]{:S(2)}) copy-start(f32[1,32,256,256]{3,0,2,1:T(1,128)S(1)} %fusion) | copy-start | bytes 25165828
  78.9 7.9 copy-start.1
  78.9 24.8 %copy-start = (f32[32,256,256]{2,1,0:T(8,128)}, f32[32,256,256]{2,1,0:T(8,128)S(1)}, u32[]{:S(2)}) copy-start(f32[32,256,256]{2,1,0:T(8,128)S(1)} %get-tuple-element.6) | copy-start | bytes 25165828
  582.1 23.4 %copy-start.3 = (f32[1,8,32,32,256]{4,2,1,3,0:T(8,128)}, f32[1,8,32,32,256]{4,2,1,3,0:T(8,128)S(1)}, u32[]{:S(2)}) copy-start(f32[1,8,32,32,256]{4,2,1,3,0:T(8,128)S(1)} %get-tuple-element.12) | copy-start | bytes 25165828
  640.5 12.0 copy-start.2
  702.5 369.4 %all-to-all-start.1 = ((f32[8,2,32,32,256]{4,2,3,1,0:T(8,128)}), f32[8,2,32,32,256]{4,2,3,1,0:T(8,128)}, u32[]{:S(2)}, u32[]{:S(2)}) async-start(f32[8,2,32,32,256]{4,2,3,1,0:T(8,128)} %fusion.68), calls=%async_computation.1 | async-start | bytes 33554432 | tf_op jit(solution)/shard_map/all_to_all | solution.py:77
  708.3 666.6 %reduce-scatter.3.cloned.1.call-start = ((), (), s32[]{:S(2)}) async-start(), calls=%async_computation.4 | async-start | bytes 20971520 | tf_op jit(solution)/shard_map/reduce_scatter | solution.py:96
  1079.7 12.9 copy-start.6
  1079.7 12.9 copy-start.4
  1105.4 21.7 %slice-start.4 = ((s8[8388608]{0:T(1024)(128)(4,1)}), s8[4194304]{0:T(1024)(128)(4,1)S(1)}, s32[]{:S(2)}) async-start(s8[8388608]{0:T(1024)(128)(4,1)} %bitcast.220), calls=%async_computation.10 | async-start | bytes 8388608
  1116.2 10.8 slice-start.5
  1127.1 14.7 copy-start.5
  1141.8 30.5 %slice-start = ((s8[8388608]{0:T(1024)(128)(4,1)}), s8[4194304]{0:T(1024)(128)(4,1)S(1)}, s32[]{:S(2)}) async-start(s8[8388608]{0:T(1024)(128)(4,1)} %bitcast.211), calls=%async_computation.6 | async-start | bytes 8388608
  1141.8 30.5 %slice-start.2 = ((s8[8388608]{0:T(1024)(128)(4,1)}), s8[4194304]{0:T(1024)(128)(4,1)S(1)}, s32[]{:S(2)}) async-start(s8[8388608]{0:T(1024)(128)(4,1)} %bitcast.213), calls=%async_computation.8 | async-start | bytes 8388608
  1156.6 15.6 slice-start.1
  1156.6 15.6 slice-start.3
  1222.1 377.7 %reduce-scatter.5.cloned.1.call-start = ((), (), s32[]{:S(2)}) async-start(), calls=%async_computation.5 | async-start | bytes 31457280 | tf_op jit(solution)/shard_map/reduce_scatter | solution.py:97
Sparse Core Ops, SparseCore 0:
  1222.2 152.6 reduce-scatter.2
  1378.0 221.7 reduce-scatter.4
